TPU v7x, 32 devices: a whole 2x2x4 slice. The times are simulated.
32 devices in a mesh: pb: 2 (over core), ka: 16 (over z, y, x).
Axes of the slice: x: 2, y: 2, z: 4, core: 2. Of those that a mesh axis runs over, the one named last changes fastest.
Arguments:
- vertex_ladder: float32 [2, 8, 1024, 1024], P(None, 'pb', 'ka'), may hold values from -6 to 6
- vertex_cross_a: float32 [2, 8, 1024, 1024], P(None, 'pb', 'ka'), may hold values from -6 to 6
- vertex_cross_b: float32 [2, 8, 1024, 1024], P(None, 'pb', 'ka'), may hold values from -6 to 6
- bubble: float32 [2, 8, 1024], P(None, 'pb'), may hold values from -0.072 to 0.072
- row_maps: int32 [2, 8, 1024], replicated, may hold values from 0 to 8191, as said below
- col_maps: int32 [2, 1024], replicated, may hold values from 0 to 1023, each once within a row
Outputs:
- ladder_out: float32 [2, 8, 1024, 1024], P(None, 'pb', 'ka')
- crossed_a: float32 [2, 8, 1024, 1024], P(None, 'pb', 'ka')
- crossed_b: float32 [2, 8, 1024, 1024], P(None, 'pb', 'ka')
Inputs may be any that keep to these rules, and one draw needn't show every extreme that they name: `row_maps`: each of the two maps is a permutation of all 8192 rows. A device holds the rows of its bosonic indices (index of pb) and its first fermionic indices (index of ka); the 256 rows of one device take exactly 8 of their source rows from each device.
All inputs are finite; a program needn't handle non-finite values.
Results may differ from a plain program's by a relative error of at most 0.007.
Values may be sent and summed in bfloat16 or wider, within the bound.
No kernel may reach another device: no remote copies, remote signals or barrier semaphores. Data moves between devices by JAX's collectives and lax.ppermute only.
A program may use at most 64 MiB of HBM per device.

v0:
```python
import jax
import jax.numpy as jnp
from jax import lax
from jax.sharding import PartitionSpec as P

LADDER = 6


def ladder_rows(vertex_rows, bubble_q, gathered):
    col_count = gathered.shape[2]
    row_count = vertex_rows.shape[1]
    right_op = jnp.concatenate([gathered[0], gathered[1]], 1)
    current = vertex_rows
    for _ in range(LADDER):
        scaled_re = current[0] * bubble_q[0][None, :] - current[1] * bubble_q[1][None, :]
        scaled_im = current[0] * bubble_q[1][None, :] + current[1] * bubble_q[0][None, :]
        left_op = jnp.concatenate([scaled_re, scaled_im], 0).astype(jnp.bfloat16)
        product = jnp.dot(left_op, right_op, preferred_element_type=jnp.float32)
        real_part = product[:row_count, :col_count] - product[row_count:, col_count:]
        imag_part = product[:row_count, col_count:] + product[row_count:, :col_count]
        current = vertex_rows + jnp.stack([real_part, imag_part])
    return current


def per_device(vertex_ladder, vertex_cross_a, vertex_cross_b, bubble, row_maps, col_maps):
    q_local = vertex_ladder.shape[1]
    row_count = vertex_ladder.shape[2]
    col_count = vertex_ladder.shape[3]
    gamma_low = vertex_ladder.astype(jnp.bfloat16)
    whole_low = lax.all_gather(gamma_low, "ka", axis=2, tiled=True)

    def per_whole(loop_state, scan_items):
        vertex_rows, gathered, bubble_q = scan_items
        return (loop_state, ladder_rows(vertex_rows, bubble_q, gathered))

    _, stacked = lax.scan(
        per_whole,
        jnp.int32(0),
        (
            jnp.moveaxis(vertex_ladder, 1, 0),
            jnp.moveaxis(whole_low, 1, 0),
            jnp.moveaxis(bubble, 1, 0),
        ),
    )
    ladder_out = jnp.moveaxis(stacked, 0, 1)
    local_count = q_local * row_count
    reducible = (ladder_out - vertex_ladder).reshape(2, local_count, col_count)
    pb_count = lax.axis_size("pb")
    ka_count = lax.axis_size("ka")
    dev_count = pb_count * ka_count
    per_peer = local_count // dev_count
    my_device = lax.axis_index("pb") * ka_count + lax.axis_index("ka")
    my_bos = lax.axis_index("pb") * q_local + jnp.arange(q_local, dtype=jnp.int32)
    my_fer = lax.axis_index("ka") * row_count + jnp.arange(row_count, dtype=jnp.int32)
    my_rows = (my_bos[:, None] * col_count + my_fer[None, :]).reshape(-1)
    slot_ids = jnp.arange(per_peer, dtype=jnp.int32)

    def device_of(global_rows):
        return global_rows // col_count // q_local * ka_count + global_rows % col_count // row_count

    def prepare(table_flat):
        by_device = (
            table_flat.reshape(pb_count, q_local, ka_count, row_count)
            .transpose(0, 2, 1, 3)
            .reshape(dev_count, local_count)
        )
        mine = (device_of(by_device) == my_device).astype(jnp.int32)
        rank = jnp.cumsum(mine, 1) - 1
        source_local = (
            by_device // col_count % q_local * row_count + by_device % col_count % row_count
        )
        hits = mine[:, :, None] * (rank[:, :, None] == slot_ids[None, None, :]).astype(jnp.int32)
        send_index = jnp.sum(hits * source_local[:, :, None], 1).reshape(-1)
        return jnp.take(reducible, send_index, axis=1)

    def place(table_flat, received, column_map):
        source = table_flat[my_rows]
        source_dev = device_of(source)
        onehot = (source_dev[:, None] == jnp.arange(dev_count, dtype=jnp.int32)[None, :]).astype(
            jnp.int32
        )
        slot_index = jnp.sum((jnp.cumsum(onehot, 0) - onehot) * onehot, 1)
        picked = jnp.take(received, source_dev * per_peer + slot_index, axis=1)
        selector = (jnp.arange(col_count, dtype=jnp.int32)[:, None] == column_map[None, :]).astype(
            jnp.float32
        )
        picked = jnp.einsum("prk,km->prm", picked, selector, precision=lax.Precision.HIGHEST)
        return picked.reshape(2, q_local, row_count, col_count)

    table_a = row_maps[0].reshape(-1)
    table_b = row_maps[1].reshape(-1)
    send_a = prepare(table_a)
    send_b = prepare(table_b)
    recv_a, recv_b = (
        lax.all_to_all(send_a, ("pb", "ka"), split_axis=1, concat_axis=1, tiled=True),
        lax.all_to_all(send_b, ("pb", "ka"), split_axis=1, concat_axis=1, tiled=True),
    )
    crossed_a = vertex_cross_a + place(table_a, recv_a, col_maps[0])
    crossed_b = vertex_cross_b + place(table_b, recv_b, col_maps[1])
    return (ladder_out, crossed_a, crossed_b)


def solution(mesh):
    return jax.shard_map(
        per_device,
        mesh=mesh,
        in_specs=(
            P(None, "pb", "ka", None),
            P(None, "pb", "ka", None),
            P(None, "pb", "ka", None),
            P(None, "pb", None),
            P(),
            P(),
        ),
        out_specs=(P(None, "pb", "ka", None), P(None, "pb", "ka", None), P(None, "pb", "ka", None)),
        check_vma=False,
    )
```

profile of v0, /device:TPU:0, one launch (start us, length us, event | category | flops | bytes accessed | tf_op | source)
XLA Modules:
  0.0 381.2 jit_solution(11262854710997987744)
XLA Ops:
  7.2 2.7 copy.84
  10.0 1.8 copy.85
  14.5 190.7 %all-gather.2.cloned.1.call-done = bf16[2,4,1024,1024]{3,2,0,1:T(8,128)(2,1)} async-done(((bf16[2,4,64,1024]{3,2,0,1:T(8,128)(2,1)}), bf16[2,4,1024,1024]{3,2,0,1:T(8,128)(2,1)}) %all-gather.2.cloned.1.call-update) | async-done | bytes 16777232 | tf_op jit(solution)/shard_map/all_gather | solution.py:30
  205.2 37.3 %while.10 = (s32[]{:T(128)}, f32[4,2,64,1024]{3,2,0,1:T(8,128)}, f32[4,2,64,1024]{3,2,1,0:T(8,128)S(1)}, f32[4,2,1024]{2,1,0:T(2,128)S(1)}, bf16[4,2,1024,1024]{...) while((s32[]{:T(128)}, f32[4,2,64,1024]{3,2,0,1:T(8,128)}, f32[4,2,64,1024]{3,2,1,0:T(8,128)S(1)}, ...), condition=%wide.region_1.2_spmd, body=%wide.region_0.1_spmd.sunk | while | flops 3280207872 | bytes 65077400 | solution.py:36
  205.3 2.7 dynamic-slice_bitcast_fusion.5
  214.6 2.7 dynamic-slice_bitcast_fusion.5
  223.9 2.7 dynamic-slice_bitcast_fusion.5
  233.2 2.7 dynamic-slice_bitcast_fusion.5
  242.4 2.6 bitcast_subtract_fusion
  246.7 4.0 %gather_fusion.2 = f32[256,2,1024]{2,1,0:T(2,128)} fusion(f32[2,256,1024]{2,0,1:T(2,128)S(1)} %bitcast.287, s32[1024]{0:T(1024)S(1)} %pad_clamp_fusion.3), kind=kCustom, calls=%fused_computation.clone | custom fusion | bytes 4195328 | tf_op jit(solution)/shard_map/jit(_take)/gather | solution.py:74
  250.7 3.6 select_bitcast_fusion.3
  254.3 3.7 all-to-all-start
  259.7 4.0 %gather_fusion.4 = f32[256,2,1024]{2,1,0:T(2,128)} fusion(f32[2,256,1024]{2,0,1:T(2,128)S(1)} %bitcast.288, s32[1024]{0:T(1024)S(1)} %pad_clamp_fusion.1), kind=kCustom, calls=%fused_computation.2.clone | custom fusion | bytes 4195328 | tf_op jit(solution)/shard_map/jit(_take)/gather | solution.py:74
  263.7 3.6 select_bitcast_fusion.1
  267.3 41.0 %all-to-all-done = f32[2,256,1024]{2,0,1:T(2,128)} async-done(((f32[2,256,1024]{2,0,1:T(2,128)}), f32[2,256,1024]{2,0,1:T(2,128)}, u32[]{:S(2)}, u32[]{:S(2)}) %all-to-all-start) | async-done | bytes 2097184 | tf_op jit(solution)/shard_map/all_to_all | solution.py:95
  308.3 2.7 all-to-all-start.1
  313.9 1.7 gather_fusion.1
  316.8 5.6 %gather_fusion.3 = f32[256,2,1024]{2,1,0:T(2,128)} fusion(f32[2,256,1024]{2,0,1:T(2,128)} %all-to-all-done, s32[1024]{0:T(1024)S(1)} %pad_clamp_fusion.2), kind=kCustom, calls=%fused_computation.1.clone | custom fusion | bytes 4195328 | tf_op jit(solution)/shard_map/jit(_take)/gather | solution.py:83
  322.5 2.6 select_bitcast_fusion.2
  325.1 4.0 %fusion.45 = f32[2,256,1024]{2,1,0:T(8,128)S(1)} fusion(f32[2,256,1024]{2,0,1:T(2,128)S(1)} %select_bitcast_fusion.2, s32[1024]{0:T(1024)S(1)} %bitcast.311), kind=kOutput, calls=%fused_computation.100 | convolution fusion | flops 6443499520 | bytes 4198400 | tf_op jit(solution)/shard_map/prk,km->prm/dot_general | solution.py:87
  330.9 30.8 %all-to-all-done.1 = f32[2,256,1024]{2,0,1:T(2,128)S(1)} async-done(((f32[2,256,1024]{2,0,1:T(2,128)}), f32[2,256,1024]{2,0,1:T(2,128)S(1)}, u32[]{:S(2)}, u32[]{:S(2)}) %all-to-all-start.1) | async-done | bytes 2097184 | tf_op jit(solution)/shard_map/all_to_all | solution.py:96
  361.7 4.0 %gather_fusion.5 = f32[256,2,1024]{2,1,0:T(2,128)} fusion(f32[2,256,1024]{2,0,1:T(2,128)S(1)} %all-to-all-done.1, s32[1024]{0:T(1024)S(1)} %pad_clamp_fusion), kind=kCustom, calls=%fused_computation.3.clone | custom fusion | bytes 4195328 | tf_op jit(solution)/shard_map/jit(_take)/gather | solution.py:83
  365.7 2.9 select_bitcast_fusion
  368.6 4.0 %fusion.48 = f32[2,256,1024]{2,1,0:T(8,128)S(1)} fusion(f32[2,256,1024]{2,0,1:T(2,128)S(1)} %select_bitcast_fusion, s32[1024]{0:T(1024)S(1)} %bitcast.310), kind=kOutput, calls=%fused_computation.102 | convolution fusion | flops 6443499520 | bytes 4198400 | tf_op jit(solution)/shard_map/prk,km->prm/dot_general | solution.py:87
  (179 shorter events, 39.4 us)
Async XLA Ops:
  7.2 198.0 %all-gather.2.cloned.1.call-start = ((), (), s32[]{:S(2)}) async-start(), calls=%async_computation.2 | async-start | bytes 17825792 | tf_op jit(solution)/shard_map/all_gather | solution.py:30
  10.0 1.8 copy-start.2
  10.0 2.4 copy-start.3
  254.3 54.1 %all-to-all-start = ((f32[2,256,1024]{2,0,1:T(2,128)}), f32[2,256,1024]{2,0,1:T(2,128)}, u32[]{:S(2)}, u32[]{:S(2)}) async-start(f32[2,256,1024]{2,0,1:T(2,128)} %select_bitcast_fusion.3), calls=%async_computation | async-start | bytes 4194304 | tf_op jit(solution)/shard_map/all_to_all | solution.py:95
  308.3 53.3 %all-to-all-start.1 = ((f32[2,256,1024]{2,0,1:T(2,128)}), f32[2,256,1024]{2,0,1:T(2,128)S(1)}, u32[]{:S(2)}, u32[]{:S(2)}) async-start(f32[2,256,1024]{2,0,1:T(2,128)} %select_bitcast_fusion.1), calls=%async_computation.1 | async-start | bytes 4194304 | tf_op jit(solution)/shard_map/all_to_all | solution.py:96
  311.1 5.7 %copy-start.4 = (s32[2,1024]{1,0:T(2,128)S(1)}, s32[2,1024]{1,0:T(2,128)}, u32[]{:S(2)}) copy-start(s32[2,1024]{1,0:T(2,128)} %param.15) | copy-start | bytes 24580
  325.1 4.0 %copy-start = (f32[2,4,64,1024]{3,2,1,0:T(8,128)S(1)}, f32[2,4,64,1024]{3,2,1,0:T(8,128)}, u32[]{:S(2)}) copy-start(f32[2,4,64,1024]{3,2,1,0:T(8,128)} %param.11) | copy-start | bytes 6291460
  368.6 4.0 %copy-start.1 = (f32[2,4,64,1024]{3,2,1,0:T(8,128)S(1)}, f32[2,4,64,1024]{3,2,1,0:T(8,128)}, u32[]{:S(2)}) copy-start(f32[2,4,64,1024]{3,2,1,0:T(8,128)} %param.12) | copy-start | bytes 6291460
Sparse Core Ops, SparseCore 0:
  11.3 193.8 all-gather.1
where the time goes:
time: 382 us; the launch traced here: 381 us
  waiting for transfers between devices  262 us (69%)
  local copies, waits for them, and re-layouts  39.7 us (10%)
  other arithmetic  32 us (8%)
  matrix products  25.6 us (7%)
  between operations  14.4 us (4%)
  starting transfers between devices  6.42 us (2%)
    all_gather x1, waiting for transfers between devices, per_device(): whole_low = lax.all_gather(gamma_low, 'ka', axis=2, tiled=True)  191 us
    all_to_all x1, waiting for transfers between devices, per_device(): lax.all_to_all(send_a, ('pb', 'ka'), split_axis=1, concat_axis=1, tiled=T...  41 us
    all_to_all x1, waiting for transfers between devices, per_device(): lax.all_to_all(send_b, ('pb', 'ka'), split_axis=1, concat_axis=1, tiled=T...  30.8 us
    dot_general x24, matrix products, ladder_rows(): product = jnp.dot(left_op, right_op, preferred_element_type=jnp.float32)  17.6 us
    squeeze x4, local copies, waits for them, and re-layouts, ladder_rows(): right_op = jnp.concatenate([gathered[0], gathered[1]], 1)  10.7 us
    gather x2, local copies, waits for them, and re-layouts, place(): picked = jnp.take(received, source_dev * per_peer + slot_index, axis=1)  9.65 us
    gather x2, local copies, waits for them, and re-layouts, prepare(): return jnp.take(reducible, send_index, axis=1)  8.05 us
    dot_general x2, matrix products, place(): jnp.einsum('prk,km->prm', picked, selector, precision=lax.Precision.HIGHEST)  8.03 us
  transfers between devices with their start and end apart: 3, of which 3 were waited for; matrix products, arithmetic and copies ran while one was open for 9% of the time, Pallas kernels for 0%

commit v1 on v0

--- a/solution.py
+++ b/solution.py
@@ -1,9 +1,37 @@
+import functools
 import jax
 import jax.numpy as jnp
 from jax import lax
 from jax.sharding import PartitionSpec as P
 
 LADDER = 6
+
+
+def view_sheets_on_mesh(mine_x, where_dim):
+    work_now = list(mine_x.shape[1:])
+    work_now[where_dim] *= mine_x.shape[0]
+    return jnp.moveaxis(mine_x, 0, where_dim).reshape(work_now)
+
+
+def stocks_apply(x_in, named_axis, on_dim):
+    size_here = lax.axis_size(named_axis)
+    tray = tuple(((to_i, (to_i + 1) % size_here) for to_i in range(size_here)))
+    taken_in, q_next = ([], [])
+    lanes = tuple(((jj, i) for i, jj in tray))
+    for idx in range(size_here - 1):
+        if idx % 2 == 0:
+            taken_in.append(
+                lax.ppermute(taken_in[-1] if taken_in else x_in, axis_name=named_axis, perm=tray)
+            )
+        else:
+            q_next.append(lax.ppermute(q_next[-1] if q_next else x_in, named_axis, lanes))
+    upper = jnp.stack([*taken_in[::-1], x_in, *q_next], axis=0)
+    p_next = lax.axis_index(named_axis) - len(taken_in)
+    upper = upper[(jnp.arange(size_here) - p_next) % size_here]
+    return view_sheets_on_mesh(upper, on_dim)
+
+
+view_wrap = functools.partial(stocks_apply, named_axis="ka", on_dim=2)
 
 
 def ladder_rows(vertex_rows, bubble_q, gathered):
@@ -27,7 +55,7 @@
     row_count = vertex_ladder.shape[2]
     col_count = vertex_ladder.shape[3]
     gamma_low = vertex_ladder.astype(jnp.bfloat16)
-    whole_low = lax.all_gather(gamma_low, "ka", axis=2, tiled=True)
+    whole_low = view_wrap(gamma_low)
 
     def per_whole(loop_state, scan_items):
         vertex_rows, gathered, bubble_q = scan_items

time: 382 us -> 597 us (1.56)
  starting transfers between devices: 6.42 us -> 172 us
  local copies, waits for them, and re-layouts: 39.7 us -> 89.9 us
  between operations: 14.4 us -> 1.34 us
    ppermute x0 -> x15, waiting for transfers between devices: none -> 194 us  [the longest x8 190 us: stocks_apply(): lax.ppermute(taken_in[-1] if taken_in else x_in, axis_name=named_axis, pe...]
    all_gather x1 -> x0, waiting for transfers between devices: 191 us -> none  [per_device(): whole_low = lax.all_gather(gamma_low, 'ka', axis=2, tiled=True)]
    ppermute x0 -> x15, starting transfers between devices: none -> 149 us  [the longest x7 108 us: stocks_apply(): lax.ppermute(q_next[-1] if q_next else x_in, named_axis, lanes)]
    unnamed x14 -> x61, local copies, waits for them, and re-layouts: 4.56 us -> 26.2 us
    all_to_all x1, starting transfers between devices: 2.73 us -> 20.6 us  [per_device(): lax.all_to_all(send_b, ('pb', 'ka'), split_axis=1, concat_axis=1, tiled=T...]
    transpose x0 -> x1, local copies, waits for them, and re-layouts: none -> 14.1 us  [view_sheets_on_mesh(): return jnp.moveaxis(mine_x, 0, where_dim).reshape(work_now)]
    gather x0 -> x1, local copies, waits for them, and re-layouts: none -> 13.4 us  [stocks_apply(): upper = upper[(jnp.arange(size_here) - p_next) % size_here]]
    all_to_all x1, waiting for transfers between devices: 30.8 us -> 42.7 us  [per_device(): lax.all_to_all(send_b, ('pb', 'ka'), split_axis=1, concat_axis=1, tiled=T...]
  transfers between devices with their start and end apart: 3 -> 17, of which waited for: 3 -> 12; matrix products, arithmetic and copies ran while one was open for 9% -> 10% of each run, Pallas kernels for 0% -> 0%
where the time goes in v1:
time: 597 us; the launch traced here: 592 us
  waiting for transfers between devices  267 us (45%)
  starting transfers between devices  172 us (29%)
  local copies, waits for them, and re-layouts  89.9 us (15%)
  other arithmetic  35 us (6%)
  matrix products  25.6 us (4%)
    ppermute x8, waiting for transfers between devices, stocks_apply(): lax.ppermute(taken_in[-1] if taken_in else x_in, axis_name=named_axis, pe...  190 us
    ppermute x7, starting transfers between devices, stocks_apply(): lax.ppermute(q_next[-1] if q_next else x_in, named_axis, lanes)  108 us
    all_to_all x1, waiting for transfers between devices, per_device(): lax.all_to_all(send_b, ('pb', 'ka'), split_axis=1, concat_axis=1, tiled=T...  42.7 us
    ppermute x8, starting transfers between devices, stocks_apply(): lax.ppermute(taken_in[-1] if taken_in else x_in, axis_name=named_axis, pe...  40.5 us
    all_to_all x1, waiting for transfers between devices, per_device(): lax.all_to_all(send_a, ('pb', 'ka'), split_axis=1, concat_axis=1, tiled=T...  30.8 us
    unnamed x61, local copies, waits for them, and re-layouts  26.2 us
    all_to_all x1, starting transfers between devices, per_device(): lax.all_to_all(send_b, ('pb', 'ka'), split_axis=1, concat_axis=1, tiled=T...  20.6 us
    dot_general x24, matrix products, ladder_rows(): product = jnp.dot(left_op, right_op, preferred_element_type=jnp.float32)  17.6 us
  transfers between devices with their start and end apart: 17, of which 12 were waited for; matrix products, arithmetic and copies ran while one was open for 10% of the time, Pallas kernels for 0%

profile of v1, /device:TPU:0, one launch (start us, length us, event | category | flops | bytes accessed | tf_op | source)
XLA Modules:
  0.0 592.1 jit_solution(17407436676142804424)
XLA Ops:
  5.4 27.2 %collective-permute-done = bf16[2,4,64,1024]{3,2,1,0:T(8,128)(2,1)S(1)} collective-permute-done((bf16[2,4,64,1024]{3,2,1,0:T(8,128)(2,1)S(1)}, bf16[2,4,64,1024]{3,2,1,0:T(8,128)(2,1)S(1)}, u32[]{:S(2)}, u32[]{:S(2)}) %collective-permute-start) | collective-permute-done | bytes 1048608 | tf_op jit(solution)/shard_map/ppermute | solution.py:24
  32.6 5.6 collective-permute-start.8
  38.2 39.0 %collective-permute-done.1 = bf16[2,4,64,1024]{3,2,1,0:T(8,128)(2,1)S(1)} collective-permute-done((bf16[2,4,64,1024]{3,2,1,0:T(8,128)(2,1)S(1)}, bf16[2,4,64,1024]{3,2,1,0:T(8,128)(2,1)S(1)}, u32[]{:S(2)}, u32[]{:S(2)}) %collective-permute-start.1) | collective-permute-done | bytes 1048608 | tf_op jit(solution)/shard_map/ppermute | solution.py:24
  80.7 24.3 %collective-permute-start.9 = (bf16[2,4,64,1024]{3,2,1,0:T(8,128)(2,1)S(1)}, bf16[2,4,64,1024]{3,2,1,0:T(8,128)(2,1)S(1)}, u32[]{:S(2)}, u32[]{:S(2)}) collective-permute-start(bf16[2,4,64,1024]{3,2,1,0:T(8,128)(2,1)S(1)} %collective-permute-done.8), channel_id=1, source_target_pairs={{1,0},{2,1},{3,2},{4,3},{5,4},{6,5},{7,6},{8,7},{9,8},{10,9},{11,1... | collective-permute-start | bytes 3145736 | tf_op jit(solution)/shard_map/ppermute | solution.py:27
  105.0 18.4 %collective-permute-done.2 = bf16[2,4,64,1024]{3,2,1,0:T(8,128)(2,1)S(1)} collective-permute-done((bf16[2,4,64,1024]{3,2,1,0:T(8,128)(2,1)S(1)}, bf16[2,4,64,1024]{3,2,1,0:T(8,128)(2,1)S(1)}, u32[]{:S(2)}, u32[]{:S(2)}) %collective-permute-start.2) | collective-permute-done | bytes 1048608 | tf_op jit(solution)/shard_map/ppermute | solution.py:24
  127.6 25.0 %collective-permute-start.10 = (bf16[2,4,64,1024]{3,2,1,0:T(8,128)(2,1)S(1)}, bf16[2,4,64,1024]{3,2,1,0:T(8,128)(2,1)S(1)}, u32[]{:S(2)}, u32[]{:S(2)}) collective-permute-start(bf16[2,4,64,1024]{3,2,1,0:T(8,128)(2,1)S(1)} %collective-permute-done.9), channel_id=1, source_target_pairs={{1,0},{2,1},{3,2},{4,3},{5,4},{6,5},{7,6},{8,7},{9,8},{10,9},{11,1... | collective-permute-start | bytes 3145736 | tf_op jit(solution)/shard_map/ppermute | solution.py:27
  152.6 17.4 %collective-permute-done.3 = bf16[2,4,64,1024]{3,2,1,0:T(8,128)(2,1)S(1)} collective-permute-done((bf16[2,4,64,1024]{3,2,1,0:T(8,128)(2,1)S(1)}, bf16[2,4,64,1024]{3,2,1,0:T(8,128)(2,1)S(1)}, u32[]{:S(2)}, u32[]{:S(2)}) %collective-permute-start.3) | collective-permute-done | bytes 1048608 | tf_op jit(solution)/shard_map/ppermute | solution.py:24
  174.3 25.0 %collective-permute-start.11 = (bf16[2,4,64,1024]{3,2,1,0:T(8,128)(2,1)S(1)}, bf16[2,4,64,1024]{3,2,1,0:T(8,128)(2,1)S(1)}, u32[]{:S(2)}, u32[]{:S(2)}) collective-permute-start(bf16[2,4,64,1024]{3,2,1,0:T(8,128)(2,1)S(1)} %collective-permute-done.10), channel_id=1, source_target_pairs={{1,0},{2,1},{3,2},{4,3},{5,4},{6,5},{7,6},{8,7},{9,8},{10,9},{11,1... | collective-permute-start | bytes 3145736 | tf_op jit(solution)/shard_map/ppermute | solution.py:27
  199.3 16.4 %collective-permute-done.4 = bf16[2,4,64,1024]{3,2,1,0:T(8,128)(2,1)} collective-permute-done((bf16[2,4,64,1024]{3,2,1,0:T(8,128)(2,1)S(1)}, bf16[2,4,64,1024]{3,2,1,0:T(8,128)(2,1)}, u32[]{:S(2)}, u32[]{:S(2)}) %collective-permute-start.4) | collective-permute-done | bytes 1048608 | tf_op jit(solution)/shard_map/ppermute | solution.py:24
  221.1 23.1 %collective-permute-start.12 = (bf16[2,4,64,1024]{3,2,1,0:T(8,128)(2,1)S(1)}, bf16[2,4,64,1024]{3,2,1,0:T(8,128)(2,1)}, u32[]{:S(2)}, u32[]{:S(2)}) collective-permute-start(bf16[2,4,64,1024]{3,2,1,0:T(8,128)(2,1)S(1)} %collective-permute-done.11), channel_id=1, source_target_pairs={{1,0},{2,1},{3,2},{4,3},{5,4},{6,5},{7,6},{8,7},{9,8},{10,9},{11,1... | collective-permute-start | bytes 3145736 | tf_op jit(solution)/shard_map/ppermute | solution.py:27
  244.3 19.1 %collective-permute-done.5 = bf16[2,4,64,1024]{3,2,1,0:T(8,128)(2,1)} collective-permute-done((bf16[2,4,64,1024]{3,2,1,0:T(8,128)(2,1)}, bf16[2,4,64,1024]{3,2,1,0:T(8,128)(2,1)}, u32[]{:S(2)}, u32[]{:S(2)}) %collective-permute-start.5) | collective-permute-done | bytes 1048608 | tf_op jit(solution)/shard_map/ppermute | solution.py:24
  263.4 25.0 %collective-permute-start.6 = (bf16[2,4,64,1024]{3,2,1,0:T(8,128)(2,1)}, bf16[2,4,64,1024]{3,2,1,0:T(8,128)(2,1)}, u32[]{:S(2)}, u32[]{:S(2)}) collective-permute-start(bf16[2,4,64,1024]{3,2,1,0:T(8,128)(2,1)} %collective-permute-done.5), channel_id=1, source_target_pairs={{0,1},{1,2},{2,3},{3,4},{4,5},{5,6},{6,7},{7,8},{8,9},{9,10},{10,1... | collective-permute-start | bytes 3145736 | tf_op jit(solution)/shard_map/ppermute | solution.py:24
  291.9 39.8 %collective-permute-done.6 = bf16[2,4,64,1024]{3,2,1,0:T(8,128)(2,1)} collective-permute-done((bf16[2,4,64,1024]{3,2,1,0:T(8,128)(2,1)}, bf16[2,4,64,1024]{3,2,1,0:T(8,128)(2,1)}, u32[]{:S(2)}, u32[]{:S(2)}) %collective-permute-start.6) | collective-permute-done | bytes 1048608 | tf_op jit(solution)/shard_map/ppermute | solution.py:24
  340.0 13.1 %collective-permute-done.7 = bf16[2,4,64,1024]{3,2,1,0:T(8,128)(2,1)} collective-permute-done((bf16[2,4,64,1024]{3,2,1,0:T(8,128)(2,1)}, bf16[2,4,64,1024]{3,2,1,0:T(8,128)(2,1)}, u32[]{:S(2)}, u32[]{:S(2)}) %collective-permute-start.7) | collective-permute-done | bytes 1048608 | tf_op jit(solution)/shard_map/ppermute | solution.py:24
  378.3 13.4 %gather_fusion = bf16[16,2,4,64,1024]{4,3,2,1,0:T(8,128)(2,1)} fusion(bf16[16,2,4,64,1024]{4,3,2,1,0:T(8,128)(2,1)} %bitcast_dynamic-update-slice_fusion, s32[1024]{0:T(1024)S(1)} %pad_clamp_fusion.5), kind=kCustom, calls=%fused_computation.4 | custom fusion | bytes 33554496 | tf_op jit(solution)/shard_map/gather | solution.py:30
  391.7 14.1 %copy.36 = bf16[2,4,16,64,1024]{4,3,2,0,1:T(8,128)(2,1)} copy(bf16[2,4,16,64,1024]{4,3,1,0,2:T(8,128)(2,1)} %bitcast.324) | data formatting | bytes 33554432 | tf_op jit(solution)/shard_map/transpose | solution.py:13
  405.7 37.3 %while.10 = (s32[]{:T(128)}, f32[4,2,64,1024]{3,2,0,1:T(8,128)}, f32[4,2,64,1024]{3,2,1,0:T(8,128)S(1)}, f32[4,2,1024]{2,1,0:T(2,128)S(1)}, bf16[4,2,1024,1024]{...) while((s32[]{:T(128)}, f32[4,2,64,1024]{3,2,0,1:T(8,128)}, f32[4,2,64,1024]{3,2,1,0:T(8,128)S(1)}, ...), condition=%wide.region_1.2_spmd, body=%wide.region_0.1_spmd.sunk | while | flops 3280207872 | bytes 65077900 | solution.py:64
  447.3 4.0 gather_fusion.5
  454.9 20.6 %all-to-all-start.1 = ((f32[2,256,1024]{2,0,1:T(2,128)}), f32[2,256,1024]{2,0,1:T(2,128)}, u32[]{:S(2)}, u32[]{:S(2)}) async-start(f32[2,256,1024]{2,0,1:T(2,128)} %select_bitcast_fusion.1), calls=%async_computation.1 | async-start | bytes 4194304 | tf_op jit(solution)/shard_map/all_to_all | solution.py:124
  475.6 4.0 gather_fusion.3
  483.2 42.7 %all-to-all-done.1 = f32[2,256,1024]{2,0,1:T(2,128)} async-done(((f32[2,256,1024]{2,0,1:T(2,128)}), f32[2,256,1024]{2,0,1:T(2,128)}, u32[]{:S(2)}, u32[]{:S(2)}) %all-to-all-start.1) | async-done | bytes 2097184 | tf_op jit(solution)/shard_map/all_to_all | solution.py:124
  534.4 5.6 gather_fusion.6
  548.4 30.8 %all-to-all-done = f32[2,256,1024]{2,0,1:T(2,128)S(1)} async-done(((f32[2,256,1024]{2,0,1:T(2,128)}), f32[2,256,1024]{2,0,1:T(2,128)S(1)}, u32[]{:S(2)}, u32[]{:S(2)}) %all-to-all-start) | async-done | bytes 2097184 | tf_op jit(solution)/shard_map/all_to_all | solution.py:123
  579.2 4.0 gather_fusion.4
  (261 shorter events, 132.6 us)
Async XLA Ops:
  0.6 217.6 %copy-start.19 = (s32[2,8,1024]{2,1,0:T(8,128)S(1)}, s32[2,8,1024]{2,1,0:T(8,128)}, u32[]{:S(2)}) copy-start(s32[2,8,1024]{2,1,0:T(8,128)} %param.14) | copy-start | bytes 196612
  2.4 30.2 %collective-permute-start = (bf16[2,4,64,1024]{3,2,1,0:T(8,128)(2,1)S(1)}, bf16[2,4,64,1024]{3,2,1,0:T(8,128)(2,1)S(1)}, u32[]{:S(2)}, u32[]{:S(2)}) collective-permute-start(bf16[2,4,64,1024]{3,2,1,0:T(8,128)(2,1)S(1)} %convert_element_type.47), channel_id=1, source_target_pairs={{0,1},{1,2},{2,3},{3,4},{4,5},{5,6},{6,7},{7,8},{8,9},{9,10},{10,1... | collective-permute-start | bytes 3145736 | tf_op jit(solution)/shard_map/ppermute | solution.py:24
  32.6 44.6 %collective-permute-start.1 = (bf16[2,4,64,1024]{3,2,1,0:T(8,128)(2,1)S(1)}, bf16[2,4,64,1024]{3,2,1,0:T(8,128)(2,1)S(1)}, u32[]{:S(2)}, u32[]{:S(2)}) collective-permute-start(bf16[2,4,64,1024]{3,2,1,0:T(8,128)(2,1)S(1)} %collective-permute-done), channel_id=1, source_target_pairs={{0,1},{1,2},{2,3},{3,4},{4,5},{5,6},{6,7},{7,8},{8,9},{9,10},{10,1... | collective-permute-start | bytes 3145736 | tf_op jit(solution)/shard_map/ppermute | solution.py:24
  32.6 47.1 %collective-permute-start.8 = (bf16[2,4,64,1024]{3,2,1,0:T(8,128)(2,1)S(1)}, bf16[2,4,64,1024]{3,2,1,0:T(8,128)(2,1)S(1)}, u32[]{:S(2)}, u32[]{:S(2)}) collective-permute-start(bf16[2,4,64,1024]{3,2,1,0:T(8,128)(2,1)S(1)} %convert_element_type.47), channel_id=1, source_target_pairs={{1,0},{2,1},{3,2},{4,3},{5,4},{6,5},{7,6},{8,7},{9,8},{10,9},{11,1... | collective-permute-start | bytes 3145736 | tf_op jit(solution)/shard_map/ppermute | solution.py:27
  77.2 50.4 %copy-start.5 = (bf16[2,4,64,1024]{3,2,1,0:T(8,128)(2,1)}, bf16[2,4,64,1024]{3,2,1,0:T(8,128)(2,1)S(1)}, u32[]{:S(2)}) copy-start(bf16[2,4,64,1024]{3,2,1,0:T(8,128)(2,1)S(1)} %collective-permute-done.1) | copy-start | bytes 3145732
  77.2 46.2 %collective-permute-start.2 = (bf16[2,4,64,1024]{3,2,1,0:T(8,128)(2,1)S(1)}, bf16[2,4,64,1024]{3,2,1,0:T(8,128)(2,1)S(1)}, u32[]{:S(2)}, u32[]{:S(2)}) collective-permute-start(bf16[2,4,64,1024]{3,2,1,0:T(8,128)(2,1)S(1)} %collective-permute-done.1), channel_id=1, source_target_pairs={{0,1},{1,2},{2,3},{3,4},{4,5},{5,6},{6,7},{7,8},{8,9},{9,10},{10,1... | collective-permute-start | bytes 3145736 | tf_op jit(solution)/shard_map/ppermute | solution.py:24
  80.7 46.9 %collective-permute-start.9 = (bf16[2,4,64,1024]{3,2,1,0:T(8,128)(2,1)S(1)}, bf16[2,4,64,1024]{3,2,1,0:T(8,128)(2,1)S(1)}, u32[]{:S(2)}, u32[]{:S(2)}) collective-permute-start(bf16[2,4,64,1024]{3,2,1,0:T(8,128)(2,1)S(1)} %collective-permute-done.8), channel_id=1, source_target_pairs={{1,0},{2,1},{3,2},{4,3},{5,4},{6,5},{7,6},{8,7},{9,8},{10,9},{11,1... | collective-permute-start | bytes 3145736 | tf_op jit(solution)/shard_map/ppermute | solution.py:27
  123.4 50.9 %copy-start.9 = (bf16[2,4,64,1024]{3,2,1,0:T(8,128)(2,1)}, bf16[2,4,64,1024]{3,2,1,0:T(8,128)(2,1)S(1)}, u32[]{:S(2)}) copy-start(bf16[2,4,64,1024]{3,2,1,0:T(8,128)(2,1)S(1)} %collective-permute-done.2) | copy-start | bytes 3145732
  123.4 46.6 %collective-permute-start.3 = (bf16[2,4,64,1024]{3,2,1,0:T(8,128)(2,1)S(1)}, bf16[2,4,64,1024]{3,2,1,0:T(8,128)(2,1)S(1)}, u32[]{:S(2)}, u32[]{:S(2)}) collective-permute-start(bf16[2,4,64,1024]{3,2,1,0:T(8,128)(2,1)S(1)} %collective-permute-done.2), channel_id=1, source_target_pairs={{0,1},{1,2},{2,3},{3,4},{4,5},{5,6},{6,7},{7,8},{8,9},{9,10},{10,1... | collective-permute-start | bytes 3145736 | tf_op jit(solution)/shard_map/ppermute | solution.py:24
  127.6 46.7 %collective-permute-start.10 = (bf16[2,4,64,1024]{3,2,1,0:T(8,128)(2,1)S(1)}, bf16[2,4,64,1024]{3,2,1,0:T(8,128)(2,1)S(1)}, u32[]{:S(2)}, u32[]{:S(2)}) collective-permute-start(bf16[2,4,64,1024]{3,2,1,0:T(8,128)(2,1)S(1)} %collective-permute-done.9), channel_id=1, source_target_pairs={{1,0},{2,1},{3,2},{4,3},{5,4},{6,5},{7,6},{8,7},{9,8},{10,9},{11,1... | collective-permute-start | bytes 3145736 | tf_op jit(solution)/shard_map/ppermute | solution.py:27
  170.0 45.6 %collective-permute-start.4 = (bf16[2,4,64,1024]{3,2,1,0:T(8,128)(2,1)S(1)}, bf16[2,4,64,1024]{3,2,1,0:T(8,128)(2,1)}, u32[]{:S(2)}, u32[]{:S(2)}) collective-permute-start(bf16[2,4,64,1024]{3,2,1,0:T(8,128)(2,1)S(1)} %collective-permute-done.3), channel_id=1, source_target_pairs={{0,1},{1,2},{2,3},{3,4},{4,5},{5,6},{6,7},{7,8},{8,9},{9,10},{10,1... | collective-permute-start | bytes 3145736 | tf_op jit(solution)/shard_map/ppermute | solution.py:24
  174.3 159.8 %copy-start.11 = (bf16[2,4,64,1024]{3,2,1,0:T(8,128)(2,1)}, bf16[2,4,64,1024]{3,2,1,0:T(8,128)(2,1)S(1)}, u32[]{:S(2)}) copy-start(bf16[2,4,64,1024]{3,2,1,0:T(8,128)(2,1)S(1)} %collective-permute-done.10) | copy-start | bytes 3145732
  174.3 46.8 %collective-permute-start.11 = (bf16[2,4,64,1024]{3,2,1,0:T(8,128)(2,1)S(1)}, bf16[2,4,64,1024]{3,2,1,0:T(8,128)(2,1)S(1)}, u32[]{:S(2)}, u32[]{:S(2)}) collective-permute-start(bf16[2,4,64,1024]{3,2,1,0:T(8,128)(2,1)S(1)} %collective-permute-done.10), channel_id=1, source_target_pairs={{1,0},{2,1},{3,2},{4,3},{5,4},{6,5},{7,6},{8,7},{9,8},{10,9},{11,1... | collective-permute-start | bytes 3145736 | tf_op jit(solution)/shard_map/ppermute | solution.py:27
  215.6 47.7 %collective-permute-start.5 = (bf16[2,4,64,1024]{3,2,1,0:T(8,128)(2,1)}, bf16[2,4,64,1024]{3,2,1,0:T(8,128)(2,1)}, u32[]{:S(2)}, u32[]{:S(2)}) collective-permute-start(bf16[2,4,64,1024]{3,2,1,0:T(8,128)(2,1)} %collective-permute-done.4), channel_id=1, source_target_pairs={{0,1},{1,2},{2,3},{3,4},{4,5},{5,6},{6,7},{7,8},{8,9},{9,10},{10,1... | collective-permute-start | bytes 3145736 | tf_op jit(solution)/shard_map/ppermute | solution.py:24
  221.1 113.0 %copy-start.13 = (bf16[2,4,64,1024]{3,2,1,0:T(8,128)(2,1)}, bf16[2,4,64,1024]{3,2,1,0:T(8,128)(2,1)S(1)}, u32[]{:S(2)}) copy-start(bf16[2,4,64,1024]{3,2,1,0:T(8,128)(2,1)S(1)} %collective-permute-done.11) | copy-start | bytes 3145732
  221.1 68.5 %collective-permute-start.12 = (bf16[2,4,64,1024]{3,2,1,0:T(8,128)(2,1)S(1)}, bf16[2,4,64,1024]{3,2,1,0:T(8,128)(2,1)}, u32[]{:S(2)}, u32[]{:S(2)}) collective-permute-start(bf16[2,4,64,1024]{3,2,1,0:T(8,128)(2,1)S(1)} %collective-permute-done.11), channel_id=1, source_target_pairs={{1,0},{2,1},{3,2},{4,3},{5,4},{6,5},{7,6},{8,7},{9,8},{10,9},{11,1... | collective-permute-start | bytes 3145736 | tf_op jit(solution)/shard_map/ppermute | solution.py:27
  263.4 68.3 %collective-permute-start.6 = (bf16[2,4,64,1024]{3,2,1,0:T(8,128)(2,1)}, bf16[2,4,64,1024]{3,2,1,0:T(8,128)(2,1)}, u32[]{:S(2)}, u32[]{:S(2)}) collective-permute-start(bf16[2,4,64,1024]{3,2,1,0:T(8,128)(2,1)} %collective-permute-done.5), channel_id=1, source_target_pairs={{0,1},{1,2},{2,3},{3,4},{4,5},{5,6},{6,7},{7,8},{8,9},{9,10},{10,1... | collective-permute-start | bytes 3145736 | tf_op jit(solution)/shard_map/ppermute | solution.py:24
  289.7 47.2 %collective-permute-start.13 = (bf16[2,4,64,1024]{3,2,1,0:T(8,128)(2,1)}, bf16[2,4,64,1024]{3,2,1,0:T(8,128)(2,1)}, u32[]{:S(2)}, u32[]{:S(2)}) collective-permute-start(bf16[2,4,64,1024]{3,2,1,0:T(8,128)(2,1)} %collective-permute-done.12), channel_id=1, source_target_pairs={{1,0},{2,1},{3,2},{4,3},{5,4},{6,5},{7,6},{8,7},{9,8},{10,9},{11,1... | collective-permute-start | bytes 3145736 | tf_op jit(solution)/shard_map/ppermute | solution.py:27
  331.7 21.5 %collective-permute-start.7 = (bf16[2,4,64,1024]{3,2,1,0:T(8,128)(2,1)}, bf16[2,4,64,1024]{3,2,1,0:T(8,128)(2,1)}, u32[]{:S(2)}, u32[]{:S(2)}) collective-permute-start(bf16[2,4,64,1024]{3,2,1,0:T(8,128)(2,1)} %collective-permute-done.6), channel_id=1, source_target_pairs={{0,1},{1,2},{2,3},{3,4},{4,5},{5,6},{6,7},{7,8},{8,9},{9,10},{10,1... | collective-permute-start | bytes 3145736 | tf_op jit(solution)/shard_map/ppermute | solution.py:24
  336.8 40.3 %collective-permute-start.14 = (bf16[2,4,64,1024]{3,2,1,0:T(8,128)(2,1)}, bf16[2,4,64,1024]{3,2,1,0:T(8,128)(2,1)S(1)}, u32[]{:S(2)}, u32[]{:S(2)}) collective-permute-start(bf16[2,4,64,1024]{3,2,1,0:T(8,128)(2,1)} %collective-permute-done.13), channel_id=1, source_target_pairs={{1,0},{2,1},{3,2},{4,3},{5,4},{6,5},{7,6},{8,7},{9,8},{10,9},{11,1... | collective-permute-start | bytes 3145736 | tf_op jit(solution)/shard_map/ppermute | solution.py:27
  454.9 71.0 %all-to-all-start.1 = ((f32[2,256,1024]{2,0,1:T(2,128)}), f32[2,256,1024]{2,0,1:T(2,128)}, u32[]{:S(2)}, u32[]{:S(2)}) async-start(f32[2,256,1024]{2,0,1:T(2,128)} %select_bitcast_fusion.1), calls=%async_computation.1 | async-start | bytes 4194304 | tf_op jit(solution)/shard_map/all_to_all | solution.py:124
  483.2 45.6 %copy-start.17 = (s32[1,8,8,128]{3,2,1,0:T(8,128)S(1)}, s32[1,8,8,128]{3,2,1,0:T(8,128)}, u32[]{:S(2)}) copy-start(s32[1,8,8,128]{3,2,1,0:T(8,128)} %get-tuple-element.74) | copy-start | bytes 98308
  483.2 45.6 %copy-start.18 = (s32[1,8,8,128]{3,2,1,0:T(8,128)S(1)}, s32[1,8,8,128]{3,2,1,0:T(8,128)}, u32[]{:S(2)}) copy-start(s32[1,8,8,128]{3,2,1,0:T(8,128)} %get-tuple-element.75) | copy-start | bytes 98308
  525.9 53.3 %all-to-all-start = ((f32[2,256,1024]{2,0,1:T(2,128)}), f32[2,256,1024]{2,0,1:T(2,128)S(1)}, u32[]{:S(2)}, u32[]{:S(2)}) async-start(f32[2,256,1024]{2,0,1:T(2,128)} %select_bitcast_fusion.3), calls=%async_computation | async-start | bytes 4194304 | tf_op jit(solution)/shard_map/all_to_all | solution.py:123
  (15 other events, 92.7 us)
